TPU v7x, 512 devices: a whole 4x4x16 slice. The times are simulated.
512 devices in a mesh: ep: 128 (over z, y, core), tp: 4 (over x).
Axes of the slice: x: 4, y: 4, z: 16, core: 2. Of those that a mesh axis runs over, the one named last changes fastest.
Arguments:
- tokens: bfloat16 [16384, 2048], P('ep', 'tp'), may hold values from -6 to 6
- cotangent: bfloat16 [16384, 2048], P('ep', 'tp'), may hold values from -6 to 6
- token_expert: int32 [16384], P('ep'), may hold values from 0 to 127, as said below
- partner: int32 [128], replicated, may hold values from 0 to 127, as said below
- gate_weight: bfloat16 [128, 768, 2048], P('ep', 'tp'), may hold values from -0.125 to 0.125
- up_weight: bfloat16 [128, 768, 2048], P('ep', 'tp'), may hold values from -0.125 to 0.125
- down_weight: bfloat16 [128, 768, 2048], P('ep', 'tp'), may hold values from -0.21875 to 0.21875
Outputs:
- token_grad: bfloat16 [16384, 2048], P('ep', 'tp')
- gate_grad: bfloat16 [128, 768, 2048], P('ep', 'tp')
- up_grad: bfloat16 [128, 768, 2048], P('ep', 'tp')
- down_grad: bfloat16 [128, 768, 2048], P('ep', 'tp')
Inputs may be any that keep to these rules, and one draw needn't show every extreme that they name: partner[partner[d]] = d and partner[d] != d: the devices of ep swap their experts in pairs. `token_expert`: each aligned block of 128 rows (the rows of one device) names each expert at most 2 times, and one expert, the same for all blocks, exactly 2 times in every block.
All inputs are finite; a program needn't handle non-finite values.
Results may differ from a plain program's by a relative error of at most 0.0049.
Values may be sent and summed in bfloat16 or wider, within the bound.
No kernel may reach another device: no remote copies, remote signals or barrier semaphores. Data moves between devices by JAX's collectives and lax.ppermute only.
A program may use at most 64 MiB of HBM per device.

v0:
```python
import jax
import jax.numpy as jnp
from jax import lax
from jax.sharding import PartitionSpec as P


def shortened(array):
    return jax.tree.map(lambda a: a.astype(jnp.bfloat16) if a.dtype == jnp.float32 else a, array)


def contract_last(left, right):
    return lax.dot_general(
        left, right, (((1,), (1,)), ((), ())), preferred_element_type=jnp.float32
    )


def contract_first(left, right):
    return lax.dot_general(
        left, right, (((0,), (0,)), ((), ())), preferred_element_type=jnp.float32
    )


def relocate(arrays, partner):
    devices = lax.axis_size("ep")
    pieces = tuple((matrix.reshape(devices, -1) for matrix in arrays))
    spread = jax.tree.map(
        lambda part, own: part.astype(own.dtype),
        lax.all_to_all(shortened(pieces), "ep", split_axis=0, concat_axis=0, tiled=True),
        pieces,
    )
    chosen = tuple((jnp.take(piece, partner, axis=0) for piece in spread))
    returned = jax.tree.map(
        lambda part, own: part.astype(own.dtype),
        lax.all_to_all(shortened(chosen), "ep", split_axis=0, concat_axis=0, tiled=True),
        chosen,
    )
    return tuple((piece.reshape(matrix.shape) for piece, matrix in zip(returned, arrays)))


def body(tokens, cotangent, token_expert, partner, gate_weight, up_weight, down_weight):
    devices = lax.axis_size("ep")
    row_count = tokens.shape[0]
    capacity = max(2, (2 * row_count + devices - 1) // devices)
    gate_weight, up_weight, down_weight = relocate((gate_weight, up_weight, down_weight), partner)
    owners = jnp.take(partner, token_expert, axis=0)
    same_owner = owners[:, None] == owners[None, :]
    earlier = jnp.arange(row_count)[:, None] > jnp.arange(row_count)[None, :]
    position = jnp.sum((same_owner & earlier).astype(jnp.int32), axis=1)
    slot_of = owners * capacity + position
    one_hot = (slot_of[None, :] == jnp.arange(devices * capacity)[:, None]).astype(jnp.bfloat16)
    send_x = jnp.dot(one_hot, tokens, preferred_element_type=jnp.float32).astype(jnp.bfloat16)
    send_g = jnp.dot(one_hot, cotangent, preferred_element_type=jnp.float32).astype(jnp.bfloat16)
    received = (
        lax.all_to_all(send_x, "ep", split_axis=0, concat_axis=0, tiled=True),
        lax.all_to_all(send_g, "ep", split_axis=0, concat_axis=0, tiled=True),
    )
    full_x, full_g = (
        lax.all_gather(received[0], "tp", axis=1, tiled=True),
        lax.all_gather(received[1], "tp", axis=1, tiled=True),
    )
    w_gate = gate_weight[0]
    w_up = up_weight[0]
    w_down = down_weight[0]
    gate = contract_last(full_x, w_gate)
    upward = contract_last(full_x, w_up)
    sigmoid_gate = jax.nn.sigmoid(gate)
    activated = gate * sigmoid_gate
    hidden = (activated * upward).astype(jnp.bfloat16)
    hidden_grad = contract_last(full_g, w_down)
    up_term = (hidden_grad * activated).astype(jnp.bfloat16)
    gate_term = (hidden_grad * upward * sigmoid_gate * (1.0 + gate * (1.0 - sigmoid_gate))).astype(
        jnp.bfloat16
    )
    partial_value = jnp.dot(gate_term, w_gate, preferred_element_type=jnp.float32) + jnp.dot(
        up_term, w_up, preferred_element_type=jnp.float32
    )
    grad_gate = contract_first(gate_term, full_x).astype(jnp.bfloat16)[None]
    grad_up = contract_first(up_term, full_x).astype(jnp.bfloat16)[None]
    grad_down = contract_first(hidden, full_g).astype(jnp.bfloat16)[None]
    share = lax.psum_scatter(partial_value, "tp", scatter_dimension=1, tiled=True).astype(
        jnp.bfloat16
    )
    coming_back = lax.all_to_all(share, "ep", split_axis=0, concat_axis=0, tiled=True)
    token_grad = contract_first(one_hot, coming_back).astype(jnp.bfloat16)
    return (token_grad, grad_gate, grad_up, grad_down)


def solution(mesh):
    in_specs = (
        P("ep", "tp"),
        P("ep", "tp"),
        P("ep"),
        P(),
        P("ep", "tp", None),
        P("ep", "tp", None),
        P("ep", "tp", None),
    )
    out_specs = (P("ep", "tp"), P("ep", "tp", None), P("ep", "tp", None), P("ep", "tp", None))
    return jax.shard_map(body, mesh=mesh, in_specs=in_specs, out_specs=out_specs, check_vma=False)
```

profile of v0, /device:TPU:33, one launch (start us, length us, event | category | flops | bytes accessed | tf_op | source)
XLA Modules:
  0.0 510.4 jit_solution(10368930947807380824)
XLA Ops:
  7.2 0.7 compare_select_fusion.1
  7.9 1.6 gather_fusion
  9.5 0.7 and_select_fusion
  10.6 0.8 all_to_all.74
  11.4 19.5 %all-to-all-start.3 = ((bf16[128,2,512]{2,1,0:T(2,128)(2,1)}), bf16[128,2,512]{2,1,0:T(2,128)(2,1)S(1)}, u32[]{:S(2)}, u32[]{:S(2)}) async-start(bf16[128,2,512]{2,1,0:T(2,128)(2,1)} %all_to_all.74), calls=%async_computation.3 | async-start | bytes 524288 | tf_op jit(solution)/shard_map/all_to_all | solution.py:54
  30.9 1.3 all_to_all.92
  32.7 5.4 %reduce.4 = bf16[128,3072]{1,0:T(8,128)(2,1)S(1)} reduce(bf16[128,1,3072]{2,1,0:T(2,128)(2,1)S(1)} %all_to_all.92, bf16[]{:T(256)} %broadcast.41), dimensions={1}, to_apply=%all_to_all.92.reduce_sub_computation | reduce | bytes 1572866 | tf_op jit(solution)/shard_map/all_to_all | solution.py:28
  38.0 1.4 reshape.104
  39.5 14.0 %all-to-all-done.3 = bf16[128,2,512]{2,1,0:T(2,128)(2,1)S(1)} async-done(((bf16[128,2,512]{2,1,0:T(2,128)(2,1)}), bf16[128,2,512]{2,1,0:T(2,128)(2,1)S(1)}, u32[]{:S(2)}, u32[]{:S(2)}) %all-to-all-start.3) | async-done | bytes 262176 | tf_op jit(solution)/shard_map/all_to_all | solution.py:54
  53.4 6.5 %all-to-all-start.6 = ((bf16[128,2,1536]{2,1,0:T(2,128)(2,1)}), bf16[128,2,1536]{2,1,0:T(2,128)(2,1)S(1)}, u32[]{:S(2)}, u32[]{:S(2)}) async-start(bf16[128,2,1536]{2,1,0:T(2,128)(2,1)} %reshape.104), calls=%async_computation.6 | async-start | bytes 1572864 | tf_op jit(solution)/shard_map/all_to_all | solution.py:28
  60.0 1.3 all_to_all.91
  61.2 5.4 %reduce.3 = bf16[128,3072]{1,0:T(8,128)(2,1)S(1)} reduce(bf16[128,1,3072]{2,1,0:T(2,128)(2,1)S(1)} %all_to_all.91, bf16[]{:T(256)} %broadcast.41), dimensions={1}, to_apply=%all_to_all.91.reduce_sub_computation | reduce | bytes 1572866 | tf_op jit(solution)/shard_map/all_to_all | solution.py:28
  66.6 1.4 reshape.112
  68.1 36.4 %all-to-all-done.6 = bf16[128,2,1536]{2,1,0:T(2,128)(2,1)S(1)} async-done(((bf16[128,2,1536]{2,1,0:T(2,128)(2,1)}), bf16[128,2,1536]{2,1,0:T(2,128)(2,1)S(1)}, u32[]{:S(2)}, u32[]{:S(2)}) %all-to-all-start.6) | async-done | bytes 786464 | tf_op jit(solution)/shard_map/all_to_all | solution.py:28
  104.5 7.2 %all-to-all-start.4 = ((bf16[128,2,1536]{2,1,0:T(2,128)(2,1)}), bf16[128,2,1536]{2,1,0:T(2,128)(2,1)}, u32[]{:S(2)}, u32[]{:S(2)}) async-start(bf16[128,2,1536]{2,1,0:T(2,128)(2,1)} %reshape.112), calls=%async_computation.4 | async-start | bytes 1572864 | tf_op jit(solution)/shard_map/all_to_all | solution.py:28
  111.7 1.3 all_to_all.90
  113.0 5.4 %reduce.5 = bf16[128,3072]{1,0:T(8,128)(2,1)S(1)} reduce(bf16[128,1,3072]{2,1,0:T(2,128)(2,1)S(1)} %all_to_all.90, bf16[]{:T(256)} %broadcast.41), dimensions={1}, to_apply=%all_to_all.90.reduce_sub_computation | reduce | bytes 1572866 | tf_op jit(solution)/shard_map/all_to_all | solution.py:28
  118.3 1.4 reshape.108
  119.8 36.0 %all-to-all-done.4 = bf16[128,2,1536]{2,1,0:T(2,128)(2,1)} async-done(((bf16[128,2,1536]{2,1,0:T(2,128)(2,1)}), bf16[128,2,1536]{2,1,0:T(2,128)(2,1)}, u32[]{:S(2)}, u32[]{:S(2)}) %all-to-all-start.4) | async-done | bytes 786464 | tf_op jit(solution)/shard_map/all_to_all | solution.py:28
  155.8 6.2 %all-to-all-start.1 = ((bf16[128,2,1536]{2,1,0:T(2,128)(2,1)}), bf16[128,2,1536]{2,1,0:T(2,128)(2,1)S(1)}, u32[]{:S(2)}, u32[]{:S(2)}) async-start(bf16[128,2,1536]{2,1,0:T(2,128)(2,1)} %reshape.108), calls=%async_computation.1 | async-start | bytes 1572864 | tf_op jit(solution)/shard_map/all_to_all | solution.py:28
  162.3 0.8 all_to_all.66
  163.1 43.6 %all-to-all-done.1 = bf16[128,2,1536]{2,1,0:T(2,128)(2,1)S(1)} async-done(((bf16[128,2,1536]{2,1,0:T(2,128)(2,1)}), bf16[128,2,1536]{2,1,0:T(2,128)(2,1)S(1)}, u32[]{:S(2)}, u32[]{:S(2)}) %all-to-all-start.1) | async-done | bytes 786464 | tf_op jit(solution)/shard_map/all_to_all | solution.py:28
  206.7 7.1 %all-to-all-start = ((bf16[128,2,512]{2,1,0:T(2,128)(2,1)}), bf16[128,2,512]{2,1,0:T(2,128)(2,1)}, u32[]{:S(2)}, u32[]{:S(2)}) async-start(bf16[128,2,512]{2,1,0:T(2,128)(2,1)} %all_to_all.66), calls=%async_computation | async-start | bytes 524288 | tf_op jit(solution)/shard_map/all_to_all | solution.py:55
  213.8 0.7 reshape.105
  214.7 5.0 reshape.113
  220.0 1.0 gather_fusion.3
  221.1 1.9 gather_fusion.2
  223.9 1.0 gather_fusion.1
  225.0 1.4 select_bitcast_fusion.1
  226.5 2.3 reduce.7
  228.8 1.4 reshape.114
  230.2 5.6 %all-to-all-done = bf16[128,2,512]{2,1,0:T(2,128)(2,1)} async-done(((bf16[128,2,512]{2,1,0:T(2,128)(2,1)}), bf16[128,2,512]{2,1,0:T(2,128)(2,1)}, u32[]{:S(2)}, u32[]{:S(2)}) %all-to-all-start) | async-done | bytes 262176 | tf_op jit(solution)/shard_map/all_to_all | solution.py:55
  235.9 10.5 %all-to-all-start.5 = ((bf16[128,2,1536]{2,1,0:T(2,128)(2,1)}), bf16[128,2,1536]{2,1,0:T(2,128)(2,1)S(1)}, u32[]{:S(2)}, u32[]{:S(2)}) async-start(bf16[128,2,1536]{2,1,0:T(2,128)(2,1)} %reshape.114), calls=%async_computation.5 | async-start | bytes 1572864 | tf_op jit(solution)/shard_map/all_to_all | solution.py:34
  246.4 1.2 reduce.8
  247.5 1.4 reshape.110
  249.0 42.0 %all-to-all-done.5 = bf16[128,2,1536]{2,1,0:T(2,128)(2,1)S(1)} async-done(((bf16[128,2,1536]{2,1,0:T(2,128)(2,1)}), bf16[128,2,1536]{2,1,0:T(2,128)(2,1)S(1)}, u32[]{:S(2)}, u32[]{:S(2)}) %all-to-all-start.5) | async-done | bytes 786464 | tf_op jit(solution)/shard_map/all_to_all | solution.py:34
  291.0 6.2 %all-to-all-start.2 = ((bf16[128,2,1536]{2,1,0:T(2,128)(2,1)}), bf16[128,2,1536]{2,1,0:T(2,128)(2,1)S(1)}, u32[]{:S(2)}, u32[]{:S(2)}) async-start(bf16[128,2,1536]{2,1,0:T(2,128)(2,1)} %reshape.110), calls=%async_computation.2 | async-start | bytes 1572864 | tf_op jit(solution)/shard_map/all_to_all | solution.py:34
  297.2 1.2 reduce.6
  298.4 1.4 reshape.106
  299.9 42.0 %all-to-all-done.2 = bf16[128,2,1536]{2,1,0:T(2,128)(2,1)S(1)} async-done(((bf16[128,2,1536]{2,1,0:T(2,128)(2,1)}), bf16[128,2,1536]{2,1,0:T(2,128)(2,1)S(1)}, u32[]{:S(2)}, u32[]{:S(2)}) %all-to-all-start.2) | async-done | bytes 786464 | tf_op jit(solution)/shard_map/all_to_all | solution.py:34
  341.9 6.6 %all-to-all-start.7 = ((bf16[128,2,1536]{2,1,0:T(2,128)(2,1)}), bf16[128,2,1536]{2,1,0:T(2,128)(2,1)}, u32[]{:S(2)}, u32[]{:S(2)}) async-start(bf16[128,2,1536]{2,1,0:T(2,128)(2,1)} %reshape.106), calls=%async_computation.7 | async-start | bytes 1572864 | tf_op jit(solution)/shard_map/all_to_all | solution.py:34
  348.6 0.8 all_to_all.76
  349.4 1.8 all_to_all.68
  351.5 0.7 reshape.115
  352.2 4.7 reduce.1
  358.7 4.7 reduce
  363.4 1.4 squeeze_reshape.9
  364.7 28.1 %all-to-all-done.7 = bf16[128,2,1536]{2,1,0:T(2,128)(2,1)} async-done(((bf16[128,2,1536]{2,1,0:T(2,128)(2,1)}), bf16[128,2,1536]{2,1,0:T(2,128)(2,1)}, u32[]{:S(2)}, u32[]{:S(2)}) %all-to-all-start.7) | async-done | bytes 786464 | tf_op jit(solution)/shard_map/all_to_all | solution.py:34
  392.9 5.3 %reshape.107 = bf16[128,1,3072]{2,1,0:T(2,128)(2,1)S(1)} reshape(bf16[128,2,1536]{2,1,0:T(2,128)(2,1)} %all-to-all-done.7) | data formatting | bytes 1572864
  398.2 4.7 reduce.2
  403.4 2.6 fusion.10
  406.0 1.2 fusion.11
  407.2 9.6 %all-gather.3.cloned.1.call-done = bf16[256,2048]{1,0:T(8,128)(2,1)} async-done(((bf16[256,512]{1,0:T(8,128)(2,1)}), bf16[256,2048]{1,0:T(8,128)(2,1)}) %all-gather.3.cloned.1.call-update) | async-done | bytes 1048592 | tf_op jit(solution)/shard_map/all_gather | solution.py:59
  416.8 1.9 multiply_convert_fusion.1
  419.3 1.8 convolution_add_fusion
  421.2 40.0 %reduce-scatter.2.cloned.1.call-done = f32[256,512]{1,0:T(8,128)} async-done(((f32[256,2048]{1,0:T(8,128)}), f32[256,512]{1,0:T(8,128)}) %reduce-scatter.2.cloned.1.call-update) | async-done | bytes 524304 | tf_op jit(solution)/shard_map/reduce_scatter | solution.py:80
  461.2 1.1 convert_element_type.39
  462.3 0.8 all_to_all.87
  463.0 16.8 %all-to-all-start.8 = ((bf16[128,2,512]{2,1,0:T(2,128)(2,1)}), bf16[128,2,512]{2,1,0:T(2,128)(2,1)S(1)}, u32[]{:S(2)}, u32[]{:S(2)}) async-start(bf16[128,2,512]{2,1,0:T(2,128)(2,1)} %all_to_all.87), calls=%async_computation.9 | async-start | bytes 524288 | tf_op jit(solution)/shard_map/all_to_all | solution.py:83
  479.9 1.3 fusion.1
  481.1 1.3 fusion
  482.4 1.3 fusion.2
  483.7 18.7 %all-to-all-done.8 = bf16[128,2,512]{2,1,0:T(2,128)(2,1)S(1)} async-done(((bf16[128,2,512]{2,1,0:T(2,128)(2,1)}), bf16[128,2,512]{2,1,0:T(2,128)(2,1)S(1)}, u32[]{:S(2)}, u32[]{:S(2)}) %all-to-all-start.8) | async-done | bytes 262176 | tf_op jit(solution)/shard_map/all_to_all | solution.py:83
  502.5 0.9 convolution_convert_fusion.5
  (67 shorter events, 6.1 us)
Async XLA Ops:
  7.2 3.2 copy-start
  7.2 23.7 %copy-start.11 = (bf16[1,192,2048]{2,1,0:T(8,128)(2,1)S(1)}, bf16[1,192,2048]{2,1,0:T(8,128)(2,1)}, u32[]{:S(2)}) copy-start(bf16[1,192,2048]{2,1,0:T(8,128)(2,1)} %param.13) | copy-start | bytes 2359300
  11.4 42.0 %all-to-all-start.3 = ((bf16[128,2,512]{2,1,0:T(2,128)(2,1)}), bf16[128,2,512]{2,1,0:T(2,128)(2,1)S(1)}, u32[]{:S(2)}, u32[]{:S(2)}) async-start(bf16[128,2,512]{2,1,0:T(2,128)(2,1)} %all_to_all.74), calls=%async_computation.3 | async-start | bytes 524288 | tf_op jit(solution)/shard_map/all_to_all | solution.py:54
  39.5 20.5 %copy-start.12 = (bf16[1,192,2048]{2,1,0:T(8,128)(2,1)S(1)}, bf16[1,192,2048]{2,1,0:T(8,128)(2,1)}, u32[]{:S(2)}) copy-start(bf16[1,192,2048]{2,1,0:T(8,128)(2,1)} %param.14) | copy-start | bytes 2359300
  53.4 51.0 %all-to-all-start.6 = ((bf16[128,2,1536]{2,1,0:T(2,128)(2,1)}), bf16[128,2,1536]{2,1,0:T(2,128)(2,1)S(1)}, u32[]{:S(2)}, u32[]{:S(2)}) async-start(bf16[128,2,1536]{2,1,0:T(2,128)(2,1)} %reshape.104), calls=%async_computation.6 | async-start | bytes 1572864 | tf_op jit(solution)/shard_map/all_to_all | solution.py:28
  68.1 43.6 %copy-start.13 = (bf16[1,192,2048]{2,1,0:T(8,128)(2,1)S(1)}, bf16[1,192,2048]{2,1,0:T(8,128)(2,1)}, u32[]{:S(2)}) copy-start(bf16[1,192,2048]{2,1,0:T(8,128)(2,1)} %param.15) | copy-start | bytes 2359300
  104.5 51.4 %all-to-all-start.4 = ((bf16[128,2,1536]{2,1,0:T(2,128)(2,1)}), bf16[128,2,1536]{2,1,0:T(2,128)(2,1)}, u32[]{:S(2)}, u32[]{:S(2)}) async-start(bf16[128,2,1536]{2,1,0:T(2,128)(2,1)} %reshape.112), calls=%async_computation.4 | async-start | bytes 1572864 | tf_op jit(solution)/shard_map/all_to_all | solution.py:28
  118.3 43.8 %copy-start.20 = (bf16[128,512]{1,0:T(8,128)(2,1)S(1)}, bf16[128,512]{1,0:T(8,128)(2,1)}, u32[]{:S(2)}) copy-start(bf16[128,512]{1,0:T(8,128)(2,1)} %param.10) | copy-start | bytes 393220
  119.8 43.3 %copy-start.1 = (s32[128]{0:T(128)S(1)}, s32[128]{0:T(128)}, u32[]{:S(2)}) copy-start(s32[128]{0:T(128)} %param.12) | copy-start | bytes 1540
  155.8 50.9 %all-to-all-start.1 = ((bf16[128,2,1536]{2,1,0:T(2,128)(2,1)}), bf16[128,2,1536]{2,1,0:T(2,128)(2,1)S(1)}, u32[]{:S(2)}, u32[]{:S(2)}) async-start(bf16[128,2,1536]{2,1,0:T(2,128)(2,1)} %reshape.108), calls=%async_computation.1 | async-start | bytes 1572864 | tf_op jit(solution)/shard_map/all_to_all | solution.py:28
  206.7 7.1 %copy-start.7 = (bf16[128,2,1536]{2,1,0:T(2,128)(2,1)}, bf16[128,2,1536]{2,1,0:T(2,128)(2,1)S(1)}, u32[]{:S(2)}) copy-start(bf16[128,2,1536]{2,1,0:T(2,128)(2,1)S(1)} %all-to-all-done.1) | copy-start | bytes 2359300
  206.7 29.1 %all-to-all-start = ((bf16[128,2,512]{2,1,0:T(2,128)(2,1)}), bf16[128,2,512]{2,1,0:T(2,128)(2,1)}, u32[]{:S(2)}, u32[]{:S(2)}) async-start(bf16[128,2,512]{2,1,0:T(2,128)(2,1)} %all_to_all.66), calls=%async_computation | async-start | bytes 524288 | tf_op jit(solution)/shard_map/all_to_all | solution.py:55
  221.1 1.9 copy-start.8
  223.9 1.1 copy-start.3
  228.8 17.6 %copy-start.4 = (bf16[128,1,3072]{2,0,1:T(8,128)(2,1)S(1)}, bf16[128,1,3072]{2,0,1:T(8,128)(2,1)}, u32[]{:S(2)}) copy-start(bf16[128,1,3072]{2,0,1:T(8,128)(2,1)} %get-tuple-element.9) | copy-start | bytes 2359300
  235.9 55.1 %all-to-all-start.5 = ((bf16[128,2,1536]{2,1,0:T(2,128)(2,1)}), bf16[128,2,1536]{2,1,0:T(2,128)(2,1)S(1)}, u32[]{:S(2)}, u32[]{:S(2)}) async-start(bf16[128,2,1536]{2,1,0:T(2,128)(2,1)} %reshape.114), calls=%async_computation.5 | async-start | bytes 1572864 | tf_op jit(solution)/shard_map/all_to_all | solution.py:34
  291.0 50.9 %all-to-all-start.2 = ((bf16[128,2,1536]{2,1,0:T(2,128)(2,1)}), bf16[128,2,1536]{2,1,0:T(2,128)(2,1)S(1)}, u32[]{:S(2)}, u32[]{:S(2)}) async-start(bf16[128,2,1536]{2,1,0:T(2,128)(2,1)} %reshape.110), calls=%async_computation.2 | async-start | bytes 1572864 | tf_op jit(solution)/shard_map/all_to_all | solution.py:34
  341.9 9.4 %copy-start.5 = (bf16[128,2,1536]{2,1,0:T(2,128)(2,1)}, bf16[128,2,1536]{2,1,0:T(2,128)(2,1)S(1)}, u32[]{:S(2)}) copy-start(bf16[128,2,1536]{2,1,0:T(2,128)(2,1)S(1)} %all-to-all-done.2) | copy-start | bytes 2359300
  341.9 51.0 %all-to-all-start.7 = ((bf16[128,2,1536]{2,1,0:T(2,128)(2,1)}), bf16[128,2,1536]{2,1,0:T(2,128)(2,1)}, u32[]{:S(2)}, u32[]{:S(2)}) async-start(bf16[128,2,1536]{2,1,0:T(2,128)(2,1)} %reshape.106), calls=%async_computation.7 | async-start | bytes 1572864 | tf_op jit(solution)/shard_map/all_to_all | solution.py:34
  348.5 54.9 %all-gather.5.cloned.1.call-start = ((), (), s32[]{:S(2)}) async-start(), calls=%async_computation.11 | async-start | bytes 1310720 | tf_op jit(solution)/shard_map/all_gather | solution.py:58
  349.4 67.4 %all-gather.3.cloned.1.call-start = ((), (), s32[]{:S(2)}) async-start(), calls=%async_computation.10 | async-start | bytes 1310720 | tf_op jit(solution)/shard_map/all_gather | solution.py:59
  351.3 109.9 %reduce-scatter.2.cloned.1.call-start = ((), (), s32[]{:S(2)}) async-start(), calls=%async_computation.12 | async-start | bytes 2621440 | tf_op jit(solution)/shard_map/reduce_scatter | solution.py:80
  356.9 1.1 copy-start.6
  403.4 13.4 %copy-start.10 = (bf16[192,2048]{1,0:T(8,128)(2,1)S(1)}, bf16[192,2048]{1,0:T(8,128)(2,1)}, u32[]{:S(2)}) copy-start(bf16[192,2048]{1,0:T(8,128)(2,1)} %squeeze_reshape.9) | copy-start | bytes 2359300
  403.4 2.6 copy-start.2
  418.7 0.6 copy-start.16
  418.7 0.7 copy-start.18
  421.1 58.7 %copy-start.19 = (bf16[256,192]{0,1:T(8,128)(2,1)S(1)}, bf16[256,192]{0,1:T(8,128)(2,1)}, u32[]{:S(2)}) copy-start(bf16[256,192]{0,1:T(8,128)(2,1)} %copy-done.18) | copy-start | bytes 294916
  462.2 18.9 %copy-start.17 = (bf16[256,192]{0,1:T(8,128)(2,1)S(1)}, bf16[256,192]{0,1:T(8,128)(2,1)}, u32[]{:S(2)}) copy-start(bf16[256,192]{0,1:T(8,128)(2,1)} %copy-done.16) | copy-start | bytes 294916
  463.0 39.4 %all-to-all-start.8 = ((bf16[128,2,512]{2,1,0:T(2,128)(2,1)}), bf16[128,2,512]{2,1,0:T(2,128)(2,1)S(1)}, u32[]{:S(2)}, u32[]{:S(2)}) async-start(bf16[128,2,512]{2,1,0:T(2,128)(2,1)} %all_to_all.87), calls=%async_computation.9 | async-start | bytes 524288 | tf_op jit(solution)/shard_map/all_to_all | solution.py:83
  479.8 2.6 copy-start.9
  479.8 2.6 copy-start.14
  479.9 2.5 copy-start.15
Sparse Core Ops, SparseCore 0:
  352.0 30.7 all-gather.4
  384.9 31.8 all-gather.2
  421.3 39.8 reduce-scatter.1
where the time goes:
time: 519 us; the launch traced here: 510 us
  waiting for transfers between devices  316 us (61%)
  starting transfers between devices  86.9 us (17%)
  local copies, waits for them, and re-layouts  40.6 us (8%)
  other arithmetic  39 us (8%)
  between operations  14.7 us (3%)
  matrix products  13 us (3%)
    all_to_all x3, waiting for transfers between devices, relocate(): lax.all_to_all(shortened(pieces), 'ep', split_axis=0, concat_axis=0, tile...  116 us
    all_to_all x3, waiting for transfers between devices, relocate(): lax.all_to_all(shortened(chosen), 'ep', split_axis=0, concat_axis=0, tile...  112 us
    reduce_scatter x1, waiting for transfers between devices, body(): lax.psum_scatter(partial_value, 'tp', scatter_dimension=1, tiled=True)  40 us
    unnamed x57, local copies, waits for them, and re-layouts  23.4 us
    all_to_all x3, starting transfers between devices, relocate(): lax.all_to_all(shortened(chosen), 'ep', split_axis=0, concat_axis=0, tile...  23.3 us
    all_to_all x7, other arithmetic, relocate(): lax.all_to_all(shortened(chosen), 'ep', split_axis=0, concat_axis=0, tile...  20.2 us
    all_to_all x3, starting transfers between devices, relocate(): lax.all_to_all(shortened(pieces), 'ep', split_axis=0, concat_axis=0, tile...  20 us
    all_to_all x1, starting transfers between devices, body(): lax.all_to_all(send_x, 'ep', split_axis=0, concat_axis=0, tiled=True)  19.5 us
  transfers between devices with their start and end apart: 12, of which 11 were waited for; matrix products, arithmetic and copies ran while one was open for 14% of the time, Pallas kernels for 0%

commit v1 on v0

v1 whole, which is shorter than its diff:
```python
import jax
import jax.numpy as jnp
from jax import lax
from jax.sharding import PartitionSpec as P


def contract_last(left, right):
    return lax.dot_general(
        left, right, (((1,), (1,)), ((), ())), preferred_element_type=jnp.float32
    )


def contract_first(left, right):
    return lax.dot_general(
        left, right, (((0,), (0,)), ((), ())), preferred_element_type=jnp.float32
    )


def exchange(array):
    devices = lax.axis_size("ep")
    rows, width = array.shape
    parts = array.reshape(devices, rows // devices, width)
    parts = lax.all_to_all(parts, "ep", split_axis=0, concat_axis=0, tiled=True)
    return parts.reshape(rows, width)


def all_features(received, width):
    stacked = jnp.concatenate([received[:, :width], received[:, width:]], axis=0)
    full = lax.all_gather(stacked, "tp", axis=1, tiled=True)
    slots = received.shape[0]
    return full[:slots], full[slots:]


def body(tokens, cotangent, token_expert, partner, gate_weight, up_weight, down_weight):
    devices = lax.axis_size("ep")
    row_count, width = tokens.shape
    capacity = max(2, (2 * row_count + devices - 1) // devices)
    slots = devices * capacity
    w_gate = gate_weight[0]
    w_up = up_weight[0]
    w_down = down_weight[0]
    hidden_count = w_gate.shape[0]

    same_expert = token_expert[:, None] == token_expert[None, :]
    earlier = jnp.arange(row_count)[:, None] > jnp.arange(row_count)[None, :]
    position = jnp.sum((same_expert & earlier).astype(jnp.int32), axis=1)
    slot_of = token_expert * capacity + position
    new_slot_of = partner.at[token_expert].get(mode="promise_in_bounds") * capacity + position
    slot_ids = jnp.arange(slots)[:, None]
    one_hot = (slot_of[None, :] == slot_ids).astype(jnp.bfloat16)
    new_one_hot = (new_slot_of[None, :] == slot_ids).astype(jnp.bfloat16)
    both = jnp.concatenate([tokens, cotangent], axis=1)
    send_old = jnp.dot(one_hot, both, preferred_element_type=jnp.float32).astype(jnp.bfloat16)
    send_new = jnp.dot(new_one_hot, both, preferred_element_type=jnp.float32).astype(jnp.bfloat16)

    received = exchange(send_old)
    send_new, received = lax.optimization_barrier((send_new, received))
    received_new = exchange(send_new)
    full_x, full_g = all_features(received, width)

    gate = contract_last(full_x, w_gate)
    upward = contract_last(full_x, w_up)
    sigmoid_gate = jax.nn.sigmoid(gate)
    activated = gate * sigmoid_gate
    hidden = (activated * upward).astype(jnp.bfloat16)
    hidden_grad = contract_last(full_g, w_down)
    up_term = (hidden_grad * activated).astype(jnp.bfloat16)
    gate_term = (
        hidden_grad * upward * sigmoid_gate * (1.0 + gate * (1.0 - sigmoid_gate))
    ).astype(jnp.bfloat16)
    partial_value = (
        jnp.dot(gate_term, w_gate, preferred_element_type=jnp.float32)
        + jnp.dot(up_term, w_up, preferred_element_type=jnp.float32)
    ).astype(jnp.bfloat16)
    terms = jnp.concatenate([gate_term, up_term, hidden], axis=1)

    share = lax.psum_scatter(partial_value, "tp", scatter_dimension=1, tiled=True)
    at_source = exchange(terms)
    onward = at_source.reshape(devices, capacity, -1).at[partner].get(mode="promise_in_bounds")
    onward = onward.reshape(slots, 3 * hidden_count)
    share, received_new = lax.optimization_barrier((share, received_new))
    new_x, new_g = all_features(received_new, width)
    arrived = exchange(jnp.concatenate([share, onward], axis=1))
    coming_back = arrived[:, :width]
    terms = arrived[:, width:]
    token_grad = contract_first(one_hot, coming_back).astype(jnp.bfloat16)
    gate_term = terms[:, :hidden_count]
    up_term = terms[:, hidden_count : 2 * hidden_count]
    hidden = terms[:, 2 * hidden_count :]
    grad_gate = contract_first(gate_term, new_x).astype(jnp.bfloat16)[None]
    grad_up = contract_first(up_term, new_x).astype(jnp.bfloat16)[None]
    grad_down = contract_first(hidden, new_g).astype(jnp.bfloat16)[None]
    return (token_grad, grad_gate, grad_up, grad_down)


def solution(mesh):
    in_specs = (
        P("ep", "tp"),
        P("ep", "tp"),
        P("ep"),
        P(),
        P("ep", "tp", None),
        P("ep", "tp", None),
        P("ep", "tp", None),
    )
    out_specs = (P("ep", "tp"), P("ep", "tp", None), P("ep", "tp", None), P("ep", "tp", None))
    return jax.shard_map(body, mesh=mesh, in_specs=in_specs, out_specs=out_specs, check_vma=False)
```

time: 519 us -> 203 us (0.39); the launches traced: 510 us -> 203 us
  waiting for transfers between devices: 316 us -> 83.9 us
  starting transfers between devices: 86.9 us -> 37.1 us
  blocking collectives: 0 us -> 42.5 us
  other arithmetic: 39 us -> 3.81 us
  local copies, waits for them, and re-layouts: 40.6 us -> 8.45 us
    all_to_all x9 -> x3, waiting for transfers between devices: 266 us -> 49.8 us  [exchange(): parts = lax.all_to_all(parts, 'ep', split_axis=0, concat_axis=0, tiled=True)]
    all_to_all x9 -> x3, starting transfers between devices: 86.6 us -> 37 us  [exchange(): parts = lax.all_to_all(parts, 'ep', split_axis=0, concat_axis=0, tiled=True)]
    all_to_all x0 -> x1, blocking collectives: none -> 42.5 us  [exchange(): parts = lax.all_to_all(parts, 'ep', split_axis=0, concat_axis=0, tiled=True)]
    all_to_all x10 -> x0, other arithmetic: 36.3 us -> none  [the longest x7 20.2 us: relocate(): lax.all_to_all(shortened(chosen), 'ep', split_axis=0, concat_axis=0, tile...]
    reduce_scatter x1, waiting for transfers between devices: 40 us -> 12.1 us  [body(): lax.psum_scatter(partial_value, 'tp', scatter_dimension=1, tiled=True)]
    unnamed x57 -> x15, local copies, waits for them, and re-layouts: 23.4 us -> 0.95 us
    all_gather x2, waiting for transfers between devices: 9.64 us -> 22 us  [all_features(): full = lax.all_gather(stacked, 'tp', axis=1, tiled=True)]
    all_to_all x10 -> x0, local copies, waits for them, and re-layouts: 9.38 us -> none  [the longest x4 4.29 us: relocate(): lax.all_to_all(shortened(pieces), 'ep', split_axis=0, concat_axis=0, tile...]
  transfers between devices with their start and end apart: 12 -> 6, of which waited for: 11 -> 5; matrix products, arithmetic and copies ran while one was open for 14% -> 6% of each run, Pallas kernels for 0% -> 0%
where the time goes in v1:
time: 203 us
  waiting for transfers between devices  83.9 us (41%)
  blocking collectives  42.5 us (21%)
  starting transfers between devices  37.1 us (18%)
  between operations  14 us (7%)
  matrix products  12.9 us (6%)
  local copies, waits for them, and re-layouts  8.45 us (4%)
  other arithmetic  3.81 us (2%)
    all_to_all x3, waiting for transfers between devices, exchange(): parts = lax.all_to_all(parts, 'ep', split_axis=0, concat_axis=0, tiled=True)  49.8 us
    all_to_all x1, blocking collectives, exchange(): parts = lax.all_to_all(parts, 'ep', split_axis=0, concat_axis=0, tiled=True)  42.5 us
    all_to_all x3, starting transfers between devices, exchange(): parts = lax.all_to_all(parts, 'ep', split_axis=0, concat_axis=0, tiled=True)  37 us
    all_gather x2, waiting for transfers between devices, all_features(): full = lax.all_gather(stacked, 'tp', axis=1, tiled=True)  22 us
    reduce_scatter x1, waiting for transfers between devices, body(): lax.psum_scatter(partial_value, 'tp', scatter_dimension=1, tiled=True)  12.1 us
    dot_general x4, matrix products, contract_first(): lax.dot_general(left, right, (((0,), (0,)), ((), ())), preferred_element_...  7.42 us
  transfers between devices with their start and end apart: 6, of which 5 were waited for; matrix products, arithmetic and copies ran while one was open for 6% of the time, Pallas kernels for 0%

profile of v1, /device:TPU:33, one launch (start us, length us, event | category | flops | bytes accessed | tf_op | source)
XLA Modules:
  0.0 202.7 jit_solution(132962404780761289)
XLA Ops:
  7.2 0.0 copy-start
  7.2 0.0 copy-start.1
  7.2 0.9 convert_reduce_fusion
  8.1 0.7 multiply_add_fusion.1
  8.8 0.9 constant_dynamic-update-slice_fusion.1
  9.7 0.9 constant_dynamic-update-slice_fusion
  10.6 0.3 convolution_convert_fusion.3
  10.9 1.0 reshape.40
  11.9 19.5 %all-to-all-start = ((bf16[128,2,1024]{2,1,0:T(2,128)(2,1)}), bf16[128,2,1024]{2,1,0:T(2,128)(2,1)S(1)}, u32[]{:S(2)}, u32[]{:S(2)}) async-start(bf16[128,2,1024]{2,1,0:T(2,128)(2,1)} %reshape.40), calls=%async_computation | async-start | bytes 1048576 | tf_op jit(solution)/shard_map/all_to_all | solution.py:23
  31.4 0.0 all-gather.3.cloned.1.call-start
  31.4 0.0 copy-done.1
  31.4 1.2 gather_fusion
  32.7 0.3 convolution_convert_fusion.4
  33.0 32.1 %all-to-all-done = bf16[128,2,1024]{2,1,0:T(2,128)(2,1)S(1)} async-done(((bf16[128,2,1024]{2,1,0:T(2,128)(2,1)}), bf16[128,2,1024]{2,1,0:T(2,128)(2,1)S(1)}, u32[]{:S(2)}, u32[]{:S(2)}) %all-to-all-start) | async-done | bytes 524320 | tf_op jit(solution)/shard_map/all_to_all | solution.py:23
  65.1 0.2 reshape.41
  65.3 0.0 copy-start.3
  65.3 0.8 pad_maximum_fusion.1
  66.2 0.0 all-gather.3.cloned.1.call-update
  66.2 0.0 copy-start.6
  66.2 1.0 reshape.42
  67.2 6.2 %all-to-all-start.1 = ((bf16[128,2,1024]{2,1,0:T(2,128)(2,1)}), bf16[128,2,1024]{2,1,0:T(2,128)(2,1)S(1)}, u32[]{:S(2)}, u32[]{:S(2)}) async-start(bf16[128,2,1024]{2,1,0:T(2,128)(2,1)} %reshape.42), calls=%async_computation.2 | async-start | bytes 1048576 | tf_op jit(solution)/shard_map/all_to_all | solution.py:23
  73.4 0.0 reduce-scatter.2.cloned.1.call-start
  73.5 22.0 %all-gather.3.cloned.1.call-done = bf16[512,2048]{1,0:T(8,128)(2,1)} async-done(((bf16[512,512]{1,0:T(8,128)(2,1)}), bf16[512,2048]{1,0:T(8,128)(2,1)}) %all-gather.3.cloned.1.call-update) | async-done | bytes 2097168 | tf_op jit(solution)/shard_map/all_gather | solution.py:29
  95.5 0.0 copy-done.3
  95.5 0.0 copy-start.5
  95.5 1.9 fusion.11
  97.4 0.0 copy-done.6
  97.4 0.0 copy-done.5
  97.4 0.5 fusion.5
  97.9 0.0 copy-done
  97.9 0.6 multiply_convert_fusion.2
  98.5 0.5 fusion.13
  98.9 1.5 fusion
  100.4 0.0 reduce-scatter.2.cloned.1.call-update
  100.5 0.2 copy.13
  100.7 0.9 reshape.44
  101.5 5.6 %all-to-all-done.1 = bf16[128,2,1024]{2,1,0:T(2,128)(2,1)S(1)} async-done(((bf16[128,2,1024]{2,1,0:T(2,128)(2,1)}), bf16[128,2,1024]{2,1,0:T(2,128)(2,1)S(1)}, u32[]{:S(2)}, u32[]{:S(2)}) %all-to-all-start.1) | async-done | bytes 524320 | tf_op jit(solution)/shard_map/all_to_all | solution.py:23
  107.1 11.3 %all-to-all-start.2 = ((bf16[128,2,576]{2,1,0:T(2,128)(2,1)}), bf16[128,2,576]{2,1,0:T(2,128)(2,1)S(1)}, u32[]{:S(2)}, u32[]{:S(2)}) async-start(bf16[128,2,576]{2,1,0:T(2,128)(2,1)} %reshape.44), calls=%async_computation.3 | async-start | bytes 655360 | tf_op jit(solution)/shard_map/all_to_all | solution.py:23
  118.4 0.0 all-gather.5.cloned.1.call-start
  118.5 0.2 reshape.43
  118.7 12.1 %reduce-scatter.2.cloned.1.call-done = bf16[256,512]{1,0:T(8,128)(2,1)} async-done(((bf16[256,2048]{1,0:T(8,128)(2,1)}), bf16[256,512]{1,0:T(8,128)(2,1)}) %reduce-scatter.2.cloned.1.call-update) | async-done | bytes 262160 | tf_op jit(solution)/shard_map/reduce_scatter | solution.py:77
  130.8 0.0 copy-start.4
  130.8 0.8 pad_maximum_fusion.2
  131.7 0.0 all-gather.5.cloned.1.call-update
  131.7 12.1 %all-to-all-done.2 = bf16[128,2,576]{2,1,0:T(2,128)(2,1)S(1)} async-done(((bf16[128,2,576]{2,1,0:T(2,128)(2,1)}), bf16[128,2,576]{2,1,0:T(2,128)(2,1)S(1)}, u32[]{:S(2)}, u32[]{:S(2)}) %all-to-all-start.2) | async-done | bytes 294944 | tf_op jit(solution)/shard_map/all_to_all | solution.py:23
  143.8 1.3 gather_fusion.1
  145.1 0.0 copy-done.4
  145.1 0.1 concatenate.20
  145.2 0.5 pad_maximum_fusion
  145.7 42.5 %all_to_all.20 = bf16[128,2,1088]{2,1,0:T(2,128)(2,1)S(1)} all-to-all(bf16[128,2,1088]{2,1,0:T(2,128)(2,1)S(1)} %pad_maximum_fusion), channel_id=1, replica_groups=mesh['ep'=128,'tp'=4] {'ep'}, dimensions={0} | all-to-all | bytes 1114112 | tf_op jit(solution)/shard_map/all_to_all | solution.py:23
  188.3 0.4 reshape.45
  188.7 0.9 convolution_convert_fusion.5
  189.6 0.0 all-gather.5.cloned.1.call-done
  189.6 0.0 copy-start.2
  189.6 2.7 %fusion.3 = bf16[1,192,2048]{2,1,0:T(8,128)(2,1)} fusion(bf16[512,2048]{1,0:T(8,128)(2,1)} %all-gather.5.cloned.1.call-done, bf16[256,1088]{1,0:T(8,128)(2,1)S(1)} %reshape.45), kind=kOutput, calls=%fused_computation.9 | convolution fusion | flops 201719808 | bytes 1966080 | tf_op jit(solution)/shard_map/dot_general | solution.py:14
  192.3 2.6 %fusion.2 = bf16[1,192,2048]{2,1,0:T(8,128)(2,1)} fusion(bf16[512,2048]{1,0:T(8,128)(2,1)} %all-gather.5.cloned.1.call-done, bf16[256,1088]{1,0:T(8,128)(2,1)S(1)} %reshape.45), kind=kOutput, calls=%fused_computation.8 | convolution fusion | flops 201719808 | bytes 1966080 | tf_op jit(solution)/shard_map/dot_general | solution.py:14
  194.9 0.0 copy-done.2
  194.9 1.3 fusion.1
  (7 shorter events, 0.1 us)
Async XLA Ops:
  7.2 90.7 %copy-start = (bf16[1,192,2048]{2,1,0:T(8,128)(2,1)S(1)}, bf16[1,192,2048]{2,1,0:T(8,128)(2,1)}, u32[]{:S(2)}) copy-start(bf16[1,192,2048]{2,1,0:T(8,128)(2,1)} %param.11) | copy-start | bytes 2359300
  7.2 24.2 %copy-start.1 = (s32[128]{0:T(128)S(1)}, s32[128]{0:T(128)}, u32[]{:S(2)}) copy-start(s32[128]{0:T(128)} %param.10) | copy-start | bytes 1540
  11.9 53.2 %all-to-all-start = ((bf16[128,2,1024]{2,1,0:T(2,128)(2,1)}), bf16[128,2,1024]{2,1,0:T(2,128)(2,1)S(1)}, u32[]{:S(2)}, u32[]{:S(2)}) async-start(bf16[128,2,1024]{2,1,0:T(2,128)(2,1)} %reshape.40), calls=%async_computation | async-start | bytes 1048576 | tf_op jit(solution)/shard_map/all_to_all | solution.py:23
  31.4 64.1 %all-gather.3.cloned.1.call-start = ((), (), s32[]{:S(2)}) async-start(), calls=%async_computation.5 | async-start | bytes 2621440 | tf_op jit(solution)/shard_map/all_gather | solution.py:29
  65.3 30.1 %copy-start.3 = (bf16[1,192,2048]{2,1,0:T(8,128)(2,1)S(1)}, bf16[1,192,2048]{2,1,0:T(8,128)(2,1)}, u32[]{:S(2)}) copy-start(bf16[1,192,2048]{2,1,0:T(8,128)(2,1)} %param.12) | copy-start | bytes 2359300
  66.2 31.2 %copy-start.6 = (bf16[1,192,2048]{2,1,0:T(8,128)(2,1)S(1)}, bf16[1,192,2048]{2,1,0:T(8,128)(2,1)}, u32[]{:S(2)}) copy-start(bf16[1,192,2048]{2,1,0:T(8,128)(2,1)} %param.13) | copy-start | bytes 2359300
  67.2 39.9 %all-to-all-start.1 = ((bf16[128,2,1024]{2,1,0:T(2,128)(2,1)}), bf16[128,2,1024]{2,1,0:T(2,128)(2,1)S(1)}, u32[]{:S(2)}, u32[]{:S(2)}) async-start(bf16[128,2,1024]{2,1,0:T(2,128)(2,1)} %reshape.42), calls=%async_computation.2 | async-start | bytes 1048576 | tf_op jit(solution)/shard_map/all_to_all | solution.py:23
  73.4 57.4 %reduce-scatter.2.cloned.1.call-start = ((), (), s32[]{:S(2)}) async-start(), calls=%async_computation.6 | async-start | bytes 1310720 | tf_op jit(solution)/shard_map/reduce_scatter | solution.py:77
  95.5 1.9 copy-start.5
  107.1 36.7 %all-to-all-start.2 = ((bf16[128,2,576]{2,1,0:T(2,128)(2,1)}), bf16[128,2,576]{2,1,0:T(2,128)(2,1)S(1)}, u32[]{:S(2)}, u32[]{:S(2)}) async-start(bf16[128,2,576]{2,1,0:T(2,128)(2,1)} %reshape.44), calls=%async_computation.3 | async-start | bytes 655360 | tf_op jit(solution)/shard_map/all_to_all | solution.py:23
  118.4 71.2 %all-gather.5.cloned.1.call-start = ((), (), s32[]{:S(2)}) async-start(), calls=%async_computation.7 | async-start | bytes 2621440 | tf_op jit(solution)/shard_map/all_gather | solution.py:29
  130.8 14.3 %copy-start.4 = (bf16[256,512]{1,0:T(8,128)(2,1)S(1)}, bf16[256,512]{1,0:T(8,128)(2,1)}, u32[]{:S(2)}) copy-start(bf16[256,512]{1,0:T(8,128)(2,1)} %reduce-scatter.2.cloned.1.call-done) | copy-start | bytes 786436
  189.6 5.3 %copy-start.2 = (bf16[512,2048]{1,0:T(8,128)(2,1)S(1)}, bf16[512,2048]{1,0:T(8,128)(2,1)}, u32[]{:S(2)}) copy-start(bf16[512,2048]{1,0:T(8,128)(2,1)} %all-gather.5.cloned.1.call-done) | copy-start | bytes 6291460
Sparse Core Ops, SparseCore 0:
  66.3 29.1 all-gather.2
  100.5 30.1 reduce-scatter.1
  133.5 39.4 all-gather.4

commit v2 on v1

v2 whole, which is shorter than its diff:
```python
import jax
import jax.numpy as jnp
from jax import lax
from jax.experimental import pallas as pl
from jax.experimental.pallas import tpu as pltpu
from jax.sharding import PartitionSpec as P


ROWS_WITH_ROWS = (((0,), (0,)), ((), ()))
LAST_WITH_LAST = (((1,), (1,)), ((), ()))


def dot(left, right, dims=(((1,), (0,)), ((), ()))):
    return lax.dot_general(left, right, dims, preferred_element_type=jnp.float32)


def by_owner(array):
    devices = lax.axis_size("ep")
    return array.reshape(devices, array.shape[0] // devices, array.shape[1])


def by_slot(parts):
    return parts.reshape(parts.shape[0] * parts.shape[1], parts.shape[2])


def exchange(parts):
    return lax.all_to_all(parts, "ep", split_axis=0, concat_axis=0, tiled=True)


def shifted(array, step):
    size = lax.axis_size("tp")
    return lax.ppermute(array, "tp", [(i, (i + step) % size) for i in range(size)])


def everyones(received, width):
    stacked = jnp.concatenate([received[:, :width], received[:, width:]], axis=0)
    steps = sorted(range(1, lax.axis_size("tp")), key=lambda k: k != 2)
    pieces = {0: stacked}
    for step in steps:
        pieces[step] = shifted(stacked, step)
    return [pieces[k] for k in range(len(pieces))]


def dispatch_kernel(expert_ref, tokens_ref, cotangent_ref, send_ref, slot_ref, *, capacity):
    count = tokens_ref.shape[0]
    width = tokens_ref.shape[1]
    slots = send_ref.shape[0]
    experts = jnp.broadcast_to(expert_ref[...], (count, count))
    same = experts == experts.T
    row = lax.broadcasted_iota(jnp.int32, (count, count), 0)
    column = lax.broadcasted_iota(jnp.int32, (count, count), 1)
    position = jnp.sum(jnp.where(same & (row < column), 1, 0), axis=0, keepdims=True)
    slot = expert_ref[...] * capacity + position
    slot_ref[...] = slot
    chosen = lax.broadcasted_iota(jnp.int32, (slots, count), 0) == slot
    one_hot = jnp.where(chosen, 1.0, 0.0).astype(jnp.bfloat16)
    send_ref[:, :width] = dot(one_hot, tokens_ref[...]).astype(jnp.bfloat16)
    send_ref[:, width:] = dot(one_hot, cotangent_ref[...]).astype(jnp.bfloat16)


def terms_kernel(place_ref, *refs, ways, slots, width):
    pieces, (gate_ref, up_ref, down_ref, terms_ref) = refs[:ways], refs[ways:]
    hidden_count = gate_ref.shape[0]
    gate = upward = hidden_grad = 0.0
    for step in range(ways):
        start = pl.multiple_of(lax.rem(place_ref[0] + ways - step, ways) * width, 128)
        features = pl.ds(start, width)
        x = pieces[step][:slots, :]
        g = pieces[step][slots:, :]
        gate = gate + dot(x, gate_ref[:, features], LAST_WITH_LAST)
        upward = upward + dot(x, up_ref[:, features], LAST_WITH_LAST)
        hidden_grad = hidden_grad + dot(g, down_ref[:, features], LAST_WITH_LAST)
    sigmoid_gate = jax.nn.sigmoid(gate)
    activated = gate * sigmoid_gate
    gate_term = hidden_grad * upward * sigmoid_gate * (1.0 + gate * (1.0 - sigmoid_gate))
    terms_ref[:, :hidden_count] = gate_term.astype(jnp.bfloat16)
    terms_ref[:, hidden_count : 2 * hidden_count] = (hidden_grad * activated).astype(jnp.bfloat16)
    terms_ref[:, 2 * hidden_count :] = (activated * upward).astype(jnp.bfloat16)


def partial_kernel(place_ref, terms_ref, gate_ref, up_ref, *outs, ways, width):
    hidden_count = gate_ref.shape[0]
    gate_term = terms_ref[:, :hidden_count]
    up_term = terms_ref[:, hidden_count : 2 * hidden_count]
    for step in range(ways):
        start = pl.multiple_of(lax.rem(place_ref[0] + step, ways) * width, 128)
        features = pl.ds(start, width)
        value = dot(gate_term, gate_ref[:, features]) + dot(up_term, up_ref[:, features])
        outs[step][...] = value.astype(outs[step].dtype)


def final_kernel(place_ref, slot_ref, arrived_ref, *refs, ways, slots, width, hidden_count):
    pieces, (token_ref, gate_ref, up_ref, down_ref) = refs[:ways], refs[ways:]
    step = pl.program_id(0)
    first = arrived_ref[:, width : width + hidden_count]
    second = arrived_ref[:, width + hidden_count : width + 2 * hidden_count]
    third = arrived_ref[:, width + 2 * hidden_count : width + 3 * hidden_count]
    for turn in range(ways):

        @pl.when(step == turn)
        def _(turn=turn):
            x = pieces[turn][:slots, :]
            g = pieces[turn][slots:, :]
            gate_ref[...] = dot(first, x, ROWS_WITH_ROWS).astype(jnp.bfloat16)
            up_ref[...] = dot(second, x, ROWS_WITH_ROWS).astype(jnp.bfloat16)
            down_ref[...] = dot(third, g, ROWS_WITH_ROWS).astype(jnp.bfloat16)
            if turn == 0:
                count = token_ref.shape[0]
                chosen = lax.broadcasted_iota(jnp.int32, (slots, count), 0) == slot_ref[...]
                one_hot = jnp.where(chosen, 1.0, 0.0).astype(jnp.bfloat16)
                back = dot(one_hot, arrived_ref[:, :width], ROWS_WITH_ROWS)
                token_ref[...] = back.astype(jnp.bfloat16)


def near(array):
    return pltpu.with_memory_space_constraint(array, pltpu.VMEM)


SMALL = pl.BlockSpec(memory_space=pltpu.SMEM)
WHOLE = pl.BlockSpec(memory_space=pltpu.VMEM)


def body(tokens, cotangent, token_expert, partner, gate_weight, up_weight, down_weight):
    devices = lax.axis_size("ep")
    ways = lax.axis_size("tp")
    row_count, width = tokens.shape
    capacity = max(2, (2 * row_count + devices - 1) // devices)
    slots = devices * capacity
    w_gate = gate_weight[0]
    w_up = up_weight[0]
    w_down = down_weight[0]
    hidden_count = w_gate.shape[0]
    place = lax.axis_index("tp").astype(jnp.int32).reshape(1)

    def shape(*dims, kind=jnp.bfloat16):
        return jax.ShapeDtypeStruct(dims, kind)

    send_old, slot_row = pl.pallas_call(
        lambda *refs: dispatch_kernel(*refs, capacity=capacity),
        out_shape=(pltpu.VMEM((slots, 2 * width), jnp.bfloat16), shape(1, row_count, kind=jnp.int32)),
        in_specs=[WHOLE] * 3,
        out_specs=(WHOLE, WHOLE),
        name="dispatch",
    )(token_expert.reshape(1, row_count), tokens, cotangent)
    received = exchange(by_owner(send_old))

    slot_of = slot_row[0]
    owners = partner.at[token_expert].get(mode="promise_in_bounds")
    new_slot_of = slot_of + (owners - token_expert) * capacity
    new_one_hot = (new_slot_of[None, :] == jnp.arange(slots)[:, None]).astype(jnp.bfloat16)
    both = jnp.concatenate([tokens, cotangent], axis=1)
    send_new = by_owner(dot(new_one_hot, both).astype(jnp.bfloat16))
    send_new, received = lax.optimization_barrier((send_new, received))
    received_new = exchange(send_new)
    pieces = everyones(by_slot(received), width)
    terms = pl.pallas_call(
        lambda *refs: terms_kernel(*refs, ways=ways, slots=slots, width=width),
        out_shape=pltpu.VMEM((slots, 3 * hidden_count), jnp.bfloat16),
        in_specs=[SMALL] + [WHOLE] * (ways + 3),
        out_specs=WHOLE,
        name="terms",
    )(place, *map(near, pieces), w_gate, w_up, w_down)
    sent, received_new = lax.optimization_barrier((by_owner(terms), received_new))
    at_source = exchange(sent)
    kinds = [jnp.float32] + [jnp.bfloat16] * (ways - 1)
    partials = pl.pallas_call(
        lambda *refs: partial_kernel(*refs, ways=ways, width=width),
        out_shape=tuple(pltpu.VMEM((slots, width), kind) for kind in kinds),
        in_specs=[SMALL] + [WHOLE] * 3,
        out_specs=(WHOLE,) * ways,
        name="partials",
    )(place, near(terms), w_gate, w_up)
    share = partials[0]
    for step in sorted(range(1, ways), key=lambda k: k != 2):
        share = share + shifted(partials[step], step).astype(jnp.float32)
    share = share.astype(jnp.bfloat16)
    onward = at_source.at[partner].get(mode="promise_in_bounds")
    share, received_new = lax.optimization_barrier((share, received_new))
    new_pieces = everyones(by_slot(received_new), width)
    arrived = by_slot(exchange(jnp.concatenate([by_owner(share), onward], axis=2)))
    turned = lambda step, place_ref: (0, lax.rem(place_ref[0] + ways - step, ways))
    fixed = lambda step, place_ref: (0, 0)
    part = pl.BlockSpec((hidden_count, width), turned)
    token_grad, grad_gate, grad_up, grad_down = pl.pallas_call(
        lambda *refs: final_kernel(
            *refs, ways=ways, slots=slots, width=width, hidden_count=hidden_count
        ),
        out_shape=(shape(row_count, width),) + (shape(hidden_count, ways * width),) * 3,
        grid_spec=pltpu.PrefetchScalarGridSpec(
            num_scalar_prefetch=1,
            grid=(ways,),
            in_specs=[WHOLE] * (2 + ways),
            out_specs=(pl.BlockSpec((row_count, width), fixed), part, part, part),
        ),
        name="final",
    )(place, slot_row, near(arrived), *map(near, new_pieces))
    return (token_grad, grad_gate[None], grad_up[None], grad_down[None])


def solution(mesh):
    in_specs = (
        P("ep", "tp"),
        P("ep", "tp"),
        P("ep"),
        P(),
        P("ep", "tp", None),
        P("ep", "tp", None),
        P("ep", "tp", None),
    )
    out_specs = (P("ep", "tp"), P("ep", "tp", None), P("ep", "tp", None), P("ep", "tp", None))
    return jax.shard_map(body, mesh=mesh, in_specs=in_specs, out_specs=out_specs, check_vma=False)
```

time: 203 us -> 197 us (0.970)
  blocking collectives: 42.5 us -> 0 us
  starting transfers between devices: 37.1 us -> 78.6 us
  waiting for transfers between devices: 83.9 us -> 97 us
  between operations: 14 us -> 0.96 us
  matrix products: 12.9 us -> 0.28 us
  Pallas kernels: 0 us -> 10.4 us
  other arithmetic: 3.81 us -> 1.6 us
    all_to_all x1 -> x0, blocking collectives: 42.5 us -> none  [exchange(): parts = lax.all_to_all(parts, 'ep', split_axis=0, concat_axis=0, tiled=True)]
    ppermute x0 -> x9, waiting for transfers between devices: none -> 31.8 us  [shifted(): lax.ppermute(array, 'tp', [(i, (i + step) % size) for i in range(size)])]
    ppermute x0 -> x9, starting transfers between devices: none -> 25.7 us  [shifted(): lax.ppermute(array, 'tp', [(i, (i + step) % size) for i in range(size)])]
    all_gather x2 -> x0, waiting for transfers between devices: 22 us -> none  [all_features(): full = lax.all_gather(stacked, 'tp', axis=1, tiled=True)]
    all_to_all x3 -> x4, starting transfers between devices: 37 us -> 52.9 us  [exchange(): return lax.all_to_all(parts, 'ep', split_axis=0, concat_axis=0, tiled=True)]
    all_to_all x3 -> x4, waiting for transfers between devices: 49.8 us -> 65.2 us  [exchange(): return lax.all_to_all(parts, 'ep', split_axis=0, concat_axis=0, tiled=True)]
    dot_general x11 -> x1, matrix products: 12.9 us -> 0.28 us  [dot(): lax.dot_general(left, right, dims, preferred_element_type=jnp.float32)]
    reduce_scatter x1 -> x0, waiting for transfers between devices: 12.1 us -> none  [body(): lax.psum_scatter(partial_value, 'tp', scatter_dimension=1, tiled=True)]
  transfers between devices with their start and end apart: 6 -> 13, of which waited for: 5 -> 8; matrix products, arithmetic and copies ran while one was open for 6% -> 3% of each run, Pallas kernels for 0% -> 2%
where the time goes in v2:
time: 197 us
  waiting for transfers between devices  97 us (49%)
  starting transfers between devices  78.6 us (40%)
  Pallas kernels  10.4 us (5%)
  local copies, waits for them, and re-layouts  7.93 us (4%)
    all_to_all x4, waiting for transfers between devices, exchange(): return lax.all_to_all(parts, 'ep', split_axis=0, concat_axis=0, tiled=True)  65.2 us
    all_to_all x4, starting transfers between devices, exchange(): return lax.all_to_all(parts, 'ep', split_axis=0, concat_axis=0, tiled=True)  52.9 us
    ppermute x9, waiting for transfers between devices, shifted(): lax.ppermute(array, 'tp', [(i, (i + step) % size) for i in range(size)])  31.8 us
    ppermute x9, starting transfers between devices, shifted(): lax.ppermute(array, 'tp', [(i, (i + step) % size) for i in range(size)])  25.7 us
  transfers between devices with their start and end apart: 13, of which 8 were waited for; matrix products, arithmetic and copies ran while one was open for 3% of the time, Pallas kernels for 2%

profile of v2, /device:TPU:33, one launch (start us, length us, event | category | flops | bytes accessed | tf_op | source)
XLA Modules:
  0.0 196.7 jit_solution(6701582096200805858)
XLA Ops:
  0.6 1.7 dispatch.1
  2.3 1.0 reshape.39
  3.3 0.0 copy-start.3
  3.3 0.0 copy-start
  3.3 0.0 copy-start.4
  3.3 0.0 copy-start.1
  3.3 0.0 copy-start.2
  3.3 19.6 %all-to-all-start = ((bf16[128,2,1024]{2,1,0:T(2,128)(2,1)}), bf16[128,2,1024]{2,1,0:T(2,128)(2,1)S(1)}, u32[]{:S(2)}, u32[]{:S(2)}) async-start(bf16[128,2,1024]{2,1,0:T(2,128)(2,1)} %reshape.39), calls=%async_computation | async-start | bytes 1048576 | tf_op jit(solution)/shard_map/all_to_all | solution.py:27
  22.9 0.0 copy-done.3
  23.0 0.0 copy-done
  23.0 1.2 gather_fusion
  24.2 0.0 copy-done.4
  24.2 0.0 copy-done.1
  24.2 0.0 copy-done.2
  24.3 0.3 convolution_convert_fusion
  24.5 1.0 reshape.38
  25.5 31.1 %all-to-all-done = bf16[128,2,1024]{2,1,0:T(2,128)(2,1)S(1)} async-done(((bf16[128,2,1024]{2,1,0:T(2,128)(2,1)}), bf16[128,2,1024]{2,1,0:T(2,128)(2,1)S(1)}, u32[]{:S(2)}, u32[]{:S(2)}) %all-to-all-start) | async-done | bytes 524320 | tf_op jit(solution)/shard_map/all_to_all | solution.py:27
  56.6 6.2 %all-to-all-start.1 = ((bf16[128,2,1024]{2,1,0:T(2,128)(2,1)}), bf16[128,2,1024]{2,1,0:T(2,128)(2,1)S(1)}, u32[]{:S(2)}, u32[]{:S(2)}) async-start(bf16[128,2,1024]{2,1,0:T(2,128)(2,1)} %reshape.38), calls=%async_computation.1 | async-start | bytes 1048576 | tf_op jit(solution)/shard_map/all_to_all | solution.py:27
  62.9 0.2 reshape.40
  63.1 4.4 %collective-permute-start.2 = (bf16[512,512]{1,0:T(8,128)(2,1)S(1)}, bf16[512,512]{1,0:T(8,128)(2,1)S(1)}, u32[]{:S(2)}, u32[]{:S(2)}) collective-permute-start(bf16[512,512]{1,0:T(8,128)(2,1)S(1)} %pad_maximum_fusion.1.refs_1_), channel_id=1, source_target_pairs={{0,3},{1,0},{2,1},{3,2},{4,7},{5,4},{6,5},{7,6},{8,11},{9,8},{10,9... | collective-permute-start | bytes 1572872 | tf_op jit(solution)/shard_map/ppermute | solution.py:32
  67.5 2.4 %collective-permute-start.1 = (bf16[512,512]{1,0:T(8,128)(2,1)S(1)}, bf16[512,512]{1,0:T(8,128)(2,1)S(1)}, u32[]{:S(2)}, u32[]{:S(2)}) collective-permute-start(bf16[512,512]{1,0:T(8,128)(2,1)S(1)} %pad_maximum_fusion.1.refs_1_), channel_id=1, source_target_pairs={{0,2},{1,3},{2,0},{3,1},{4,6},{5,7},{6,4},{7,5},{8,10},{9,11},{10,... | collective-permute-start | bytes 1572872 | tf_op jit(solution)/shard_map/ppermute | solution.py:32
  70.0 2.5 %collective-permute-start = (bf16[512,512]{1,0:T(8,128)(2,1)S(1)}, bf16[512,512]{1,0:T(8,128)(2,1)S(1)}, u32[]{:S(2)}, u32[]{:S(2)}) collective-permute-start(bf16[512,512]{1,0:T(8,128)(2,1)S(1)} %pad_maximum_fusion.1.refs_1_), channel_id=1, source_target_pairs={{0,1},{1,2},{2,3},{3,0},{4,5},{5,6},{6,7},{7,4},{8,9},{9,10},{10,1... | collective-permute-start | bytes 1572872 | tf_op jit(solution)/shard_map/ppermute | solution.py:32
  72.5 6.6 %collective-permute-done.2.refs_4_ = bf16[512,512]{1,0:T(8,128)(2,1)S(1)} collective-permute-done((bf16[512,512]{1,0:T(8,128)(2,1)S(1)}, bf16[512,512]{1,0:T(8,128)(2,1)S(1)}, u32[]{:S(2)}, u32[]{:S(2)}) %collective-permute-start.2) | collective-permute-done | bytes 524320 | tf_op jit(solution)/shard_map/ppermute | solution.py:32
  79.1 4.7 %collective-permute-done.1.refs_3_ = bf16[512,512]{1,0:T(8,128)(2,1)S(1)} collective-permute-done((bf16[512,512]{1,0:T(8,128)(2,1)S(1)}, bf16[512,512]{1,0:T(8,128)(2,1)S(1)}, u32[]{:S(2)}, u32[]{:S(2)}) %collective-permute-start.1) | collective-permute-done | bytes 524320 | tf_op jit(solution)/shard_map/ppermute | solution.py:32
  83.8 12.2 %collective-permute-done.refs_2_ = bf16[512,512]{1,0:T(8,128)(2,1)S(1)} collective-permute-done((bf16[512,512]{1,0:T(8,128)(2,1)S(1)}, bf16[512,512]{1,0:T(8,128)(2,1)S(1)}, u32[]{:S(2)}, u32[]{:S(2)}) %collective-permute-start) | collective-permute-done | bytes 524320 | tf_op jit(solution)/shard_map/ppermute | solution.py:32
  96.0 2.7 %terms.1.refs_1_ = bf16[256,576]{1,0:T(8,128)(2,1)S(1)} custom-call(s32[1]{0:T(128)} %bitcast.refs_0_, bf16[512,512]{1,0:T(8,128)(2,1)S(1)} %pad_maximum_fusion.1.refs_1_, bf16[512,512]{1,0:T(8,128)(2,1)S(1)} %collective-permute-done.refs_2_, bf16[512,512]{1,0:T(8,128)(2,1)S(1)} %collective-permute-done.1.refs_3_, ...), custom_call_target="tpu_custom_call" | custom-call | tf_op jit(solution)/shard_map/terms/pallas_call | solution.py:156
  98.7 0.9 reshape.41
  99.6 0.0 all-to-all-done.1
  99.6 16.2 %all-to-all-start.2 = ((bf16[128,2,576]{2,1,0:T(2,128)(2,1)}), bf16[128,2,576]{2,1,0:T(2,128)(2,1)S(1)}, u32[]{:S(2)}, u32[]{:S(2)}) async-start(bf16[128,2,576]{2,1,0:T(2,128)(2,1)} %reshape.41), calls=%async_computation.2 | async-start | bytes 655360 | tf_op jit(solution)/shard_map/all_to_all | solution.py:27
  115.8 2.1 %partials.1 = (f32[256,512]{1,0:T(8,128)S(1)}, bf16[256,512]{1,0:T(8,128)(2,1)S(1)}, bf16[256,512]{1,0:T(8,128)(2,1)S(1)}, bf16[256,512]{1,0:T(8,128)(2,1)S(1)}) custom-call(s32[1]{0:T(128)} %bitcast.refs_0_, bf16[256,576]{1,0:T(8,128)(2,1)S(1)} %terms.1.refs_1_, bf16[192,2048]{1,0:T(8,128)(2,1)} %bitcast.11, bf16[192,2048]{1,0:T(8,128)(2,1)} %bitcast.13), custom_call_target="tpu_custom_call" | custom-call | tf_op jit(solution)/shard_map/partials/pallas_call | solution.py:166
  117.9 2.4 %collective-permute-start.3 = (bf16[256,512]{1,0:T(8,128)(2,1)S(1)}, bf16[256,512]{1,0:T(8,128)(2,1)S(1)}, u32[]{:S(2)}, u32[]{:S(2)}) collective-permute-start(bf16[256,512]{1,0:T(8,128)(2,1)S(1)} %get-tuple-element.24), channel_id=1, source_target_pairs={{0,2},{1,3},{2,0},{3,1},{4,6},{5,7},{6,4},{7,5},{8,10},{9,11},{10,... | collective-permute-start | bytes 786440 | tf_op jit(solution)/shard_map/ppermute | solution.py:32
  120.4 2.3 %collective-permute-start.4 = (bf16[256,512]{1,0:T(8,128)(2,1)S(1)}, bf16[256,512]{1,0:T(8,128)(2,1)S(1)}, u32[]{:S(2)}, u32[]{:S(2)}) collective-permute-start(bf16[256,512]{1,0:T(8,128)(2,1)S(1)} %get-tuple-element.25), channel_id=1, source_target_pairs={{0,1},{1,2},{2,3},{3,0},{4,5},{5,6},{6,7},{7,4},{8,9},{9,10},{10,1... | collective-permute-start | bytes 786440 | tf_op jit(solution)/shard_map/ppermute | solution.py:32
  122.7 4.2 %collective-permute-start.5 = (bf16[256,512]{1,0:T(8,128)(2,1)S(1)}, bf16[256,512]{1,0:T(8,128)(2,1)S(1)}, u32[]{:S(2)}, u32[]{:S(2)}) collective-permute-start(bf16[256,512]{1,0:T(8,128)(2,1)S(1)} %get-tuple-element.26), channel_id=1, source_target_pairs={{0,3},{1,0},{2,1},{3,2},{4,7},{5,4},{6,5},{7,6},{8,11},{9,8},{10,9... | collective-permute-start | bytes 786440 | tf_op jit(solution)/shard_map/ppermute | solution.py:32
  126.9 1.9 collective-permute-done.3
  128.8 6.3 %collective-permute-done.4 = bf16[256,512]{1,0:T(8,128)(2,1)S(1)} collective-permute-done((bf16[256,512]{1,0:T(8,128)(2,1)S(1)}, bf16[256,512]{1,0:T(8,128)(2,1)S(1)}, u32[]{:S(2)}, u32[]{:S(2)}) %collective-permute-start.4) | collective-permute-done | bytes 262176 | tf_op jit(solution)/shard_map/ppermute | solution.py:32
  135.2 0.0 collective-permute-done.5
  135.2 0.1 add_convert_fusion
  135.3 0.1 reshape.42
  135.4 5.7 %all-to-all-done.2 = bf16[128,2,576]{2,1,0:T(2,128)(2,1)S(1)} async-done(((bf16[128,2,576]{2,1,0:T(2,128)(2,1)}), bf16[128,2,576]{2,1,0:T(2,128)(2,1)S(1)}, u32[]{:S(2)}, u32[]{:S(2)}) %all-to-all-start.2) | async-done | bytes 294944 | tf_op jit(solution)/shard_map/all_to_all | solution.py:27
  141.2 1.3 gather_fusion.1
  142.4 1.4 pad_maximum_fusion
  143.8 10.9 %all-to-all-start.3 = ((bf16[128,2,1088]{2,1,0:T(2,128)(2,1)}), bf16[128,2,1088]{2,1,0:T(2,128)(2,1)}, u32[]{:S(2)}, u32[]{:S(2)}) async-start(bf16[128,2,1088]{2,1,0:T(2,128)(2,1)} %pad_maximum_fusion), calls=%async_computation.3 | async-start | bytes 1179648 | tf_op jit(solution)/shard_map/all_to_all | solution.py:27
  154.7 0.2 reshape.44
  155.0 3.0 %collective-permute-start.8 = (bf16[512,512]{1,0:T(8,128)(2,1)S(1)}, bf16[512,512]{1,0:T(8,128)(2,1)S(1)}, u32[]{:S(2)}, u32[]{:S(2)}) collective-permute-start(bf16[512,512]{1,0:T(8,128)(2,1)S(1)} %pad_maximum_fusion.2.refs_3_), channel_id=1, source_target_pairs={{0,3},{1,0},{2,1},{3,2},{4,7},{5,4},{6,5},{7,6},{8,11},{9,8},{10,9... | collective-permute-start | bytes 1572872 | tf_op jit(solution)/shard_map/ppermute | solution.py:32
  158.0 1.9 collective-permute-start.7
  160.0 2.5 %collective-permute-start.6 = (bf16[512,512]{1,0:T(8,128)(2,1)S(1)}, bf16[512,512]{1,0:T(8,128)(2,1)S(1)}, u32[]{:S(2)}, u32[]{:S(2)}) collective-permute-start(bf16[512,512]{1,0:T(8,128)(2,1)S(1)} %pad_maximum_fusion.2.refs_3_), channel_id=1, source_target_pairs={{0,1},{1,2},{2,3},{3,0},{4,5},{5,6},{6,7},{7,4},{8,9},{9,10},{10,1... | collective-permute-start | bytes 1572872 | tf_op jit(solution)/shard_map/ppermute | solution.py:32
  162.4 28.3 %all-to-all-done.3 = bf16[128,2,1088]{2,1,0:T(2,128)(2,1)} async-done(((bf16[128,2,1088]{2,1,0:T(2,128)(2,1)}), bf16[128,2,1088]{2,1,0:T(2,128)(2,1)}, u32[]{:S(2)}, u32[]{:S(2)}) %all-to-all-start.3) | async-done | bytes 557088 | tf_op jit(solution)/shard_map/all_to_all | solution.py:27
  190.8 2.0 %reshape.43.refs_2_ = bf16[256,1088]{1,0:T(8,128)(2,1)S(1)} reshape(bf16[128,2,1088]{2,1,0:T(2,128)(2,1)} %all-to-all-done.3) | data formatting | bytes 1114112 | tf_op jit(solution)/shard_map/reshape | solution.py:23
  192.7 0.0 collective-permute-done.8.refs_6_
  192.7 0.0 collective-permute-done.7.refs_5_
  192.8 0.0 collective-permute-done.6.refs_4_
  192.8 3.9 %final.1 = (bf16[128,512]{1,0:T(8,128)(2,1)}, bf16[192,2048]{1,0:T(8,128)(2,1)}, bf16[192,2048]{1,0:T(8,128)(2,1)}, bf16[192,2048]{1,0:T(8,128)(2,1)}) custom-call(s32[1]{0:T(128)} %bitcast.refs_0_, s32[1,128]{1,0:T(1,128)} %get-tuple-element.20.refs_1_, bf16[256,1088]{1,0:T(8,128)(2,1)S(1)} %reshape.43.refs_2_, ...), custom_call_target="tpu_custom_call" | custom-call | tf_op jit(solution)/shard_map/final/pallas_call | solution.py:184
  (9 shorter events, 0.2 us)
Async XLA Ops:
  3.3 19.6 %copy-start.3 = (s32[128]{0:T(128)S(1)}, s32[128]{0:T(128)}, u32[]{:S(2)}) copy-start(s32[128]{0:T(128)} %param.9) | copy-start | bytes 1540
  3.3 19.7 %copy-start = (s32[128]{0:T(128)S(1)}, s32[128]{0:T(128)}, u32[]{:S(2)}) copy-start(s32[128]{0:T(128)} %param.10) | copy-start | bytes 1540
  3.3 20.9 %copy-start.4 = (s32[1,128]{1,0:T(1,128)S(1)}, s32[1,128]{1,0:T(1,128)}, u32[]{:S(2)}) copy-start(s32[1,128]{1,0:T(1,128)} %get-tuple-element.20.refs_1_) | copy-start | bytes 1540
  3.3 20.9 %copy-start.1 = (bf16[128,512]{1,0:T(8,128)(2,1)S(1)}, bf16[128,512]{1,0:T(8,128)(2,1)}, u32[]{:S(2)}) copy-start(bf16[128,512]{1,0:T(8,128)(2,1)} %refs_1_.1) | copy-start | bytes 393220
  3.3 20.9 %copy-start.2 = (bf16[128,512]{1,0:T(8,128)(2,1)S(1)}, bf16[128,512]{1,0:T(8,128)(2,1)}, u32[]{:S(2)}) copy-start(bf16[128,512]{1,0:T(8,128)(2,1)} %refs_2_.1) | copy-start | bytes 393220
  3.3 53.3 %all-to-all-start = ((bf16[128,2,1024]{2,1,0:T(2,128)(2,1)}), bf16[128,2,1024]{2,1,0:T(2,128)(2,1)S(1)}, u32[]{:S(2)}, u32[]{:S(2)}) async-start(bf16[128,2,1024]{2,1,0:T(2,128)(2,1)} %reshape.39), calls=%async_computation | async-start | bytes 1048576 | tf_op jit(solution)/shard_map/all_to_all | solution.py:27
  56.6 42.9 %all-to-all-start.1 = ((bf16[128,2,1024]{2,1,0:T(2,128)(2,1)}), bf16[128,2,1024]{2,1,0:T(2,128)(2,1)S(1)}, u32[]{:S(2)}, u32[]{:S(2)}) async-start(bf16[128,2,1024]{2,1,0:T(2,128)(2,1)} %reshape.38), calls=%async_computation.1 | async-start | bytes 1048576 | tf_op jit(solution)/shard_map/all_to_all | solution.py:27
  63.1 16.0 %collective-permute-start.2 = (bf16[512,512]{1,0:T(8,128)(2,1)S(1)}, bf16[512,512]{1,0:T(8,128)(2,1)S(1)}, u32[]{:S(2)}, u32[]{:S(2)}) collective-permute-start(bf16[512,512]{1,0:T(8,128)(2,1)S(1)} %pad_maximum_fusion.1.refs_1_), channel_id=1, source_target_pairs={{0,3},{1,0},{2,1},{3,2},{4,7},{5,4},{6,5},{7,6},{8,11},{9,8},{10,9... | collective-permute-start | bytes 1572872 | tf_op jit(solution)/shard_map/ppermute | solution.py:32
  67.5 16.2 %collective-permute-start.1 = (bf16[512,512]{1,0:T(8,128)(2,1)S(1)}, bf16[512,512]{1,0:T(8,128)(2,1)S(1)}, u32[]{:S(2)}, u32[]{:S(2)}) collective-permute-start(bf16[512,512]{1,0:T(8,128)(2,1)S(1)} %pad_maximum_fusion.1.refs_1_), channel_id=1, source_target_pairs={{0,2},{1,3},{2,0},{3,1},{4,6},{5,7},{6,4},{7,5},{8,10},{9,11},{10,... | collective-permute-start | bytes 1572872 | tf_op jit(solution)/shard_map/ppermute | solution.py:32
  70.0 26.0 %collective-permute-start = (bf16[512,512]{1,0:T(8,128)(2,1)S(1)}, bf16[512,512]{1,0:T(8,128)(2,1)S(1)}, u32[]{:S(2)}, u32[]{:S(2)}) collective-permute-start(bf16[512,512]{1,0:T(8,128)(2,1)S(1)} %pad_maximum_fusion.1.refs_1_), channel_id=1, source_target_pairs={{0,1},{1,2},{2,3},{3,0},{4,5},{5,6},{6,7},{7,4},{8,9},{9,10},{10,1... | collective-permute-start | bytes 1572872 | tf_op jit(solution)/shard_map/ppermute | solution.py:32
  99.6 41.6 %all-to-all-start.2 = ((bf16[128,2,576]{2,1,0:T(2,128)(2,1)}), bf16[128,2,576]{2,1,0:T(2,128)(2,1)S(1)}, u32[]{:S(2)}, u32[]{:S(2)}) async-start(bf16[128,2,576]{2,1,0:T(2,128)(2,1)} %reshape.41), calls=%async_computation.2 | async-start | bytes 655360 | tf_op jit(solution)/shard_map/all_to_all | solution.py:27
  117.9 10.9 %collective-permute-start.3 = (bf16[256,512]{1,0:T(8,128)(2,1)S(1)}, bf16[256,512]{1,0:T(8,128)(2,1)S(1)}, u32[]{:S(2)}, u32[]{:S(2)}) collective-permute-start(bf16[256,512]{1,0:T(8,128)(2,1)S(1)} %get-tuple-element.24), channel_id=1, source_target_pairs={{0,2},{1,3},{2,0},{3,1},{4,6},{5,7},{6,4},{7,5},{8,10},{9,11},{10,... | collective-permute-start | bytes 786440 | tf_op jit(solution)/shard_map/ppermute | solution.py:32
  120.4 14.8 %collective-permute-start.4 = (bf16[256,512]{1,0:T(8,128)(2,1)S(1)}, bf16[256,512]{1,0:T(8,128)(2,1)S(1)}, u32[]{:S(2)}, u32[]{:S(2)}) collective-permute-start(bf16[256,512]{1,0:T(8,128)(2,1)S(1)} %get-tuple-element.25), channel_id=1, source_target_pairs={{0,1},{1,2},{2,3},{3,0},{4,5},{5,6},{6,7},{7,4},{8,9},{9,10},{10,1... | collective-permute-start | bytes 786440 | tf_op jit(solution)/shard_map/ppermute | solution.py:32
  122.7 12.5 %collective-permute-start.5 = (bf16[256,512]{1,0:T(8,128)(2,1)S(1)}, bf16[256,512]{1,0:T(8,128)(2,1)S(1)}, u32[]{:S(2)}, u32[]{:S(2)}) collective-permute-start(bf16[256,512]{1,0:T(8,128)(2,1)S(1)} %get-tuple-element.26), channel_id=1, source_target_pairs={{0,3},{1,0},{2,1},{3,2},{4,7},{5,4},{6,5},{7,6},{8,11},{9,8},{10,9... | collective-permute-start | bytes 786440 | tf_op jit(solution)/shard_map/ppermute | solution.py:32
  143.8 46.9 %all-to-all-start.3 = ((bf16[128,2,1088]{2,1,0:T(2,128)(2,1)}), bf16[128,2,1088]{2,1,0:T(2,128)(2,1)}, u32[]{:S(2)}, u32[]{:S(2)}) async-start(bf16[128,2,1088]{2,1,0:T(2,128)(2,1)} %pad_maximum_fusion), calls=%async_computation.3 | async-start | bytes 1179648 | tf_op jit(solution)/shard_map/all_to_all | solution.py:27
  155.0 37.7 %collective-permute-start.8 = (bf16[512,512]{1,0:T(8,128)(2,1)S(1)}, bf16[512,512]{1,0:T(8,128)(2,1)S(1)}, u32[]{:S(2)}, u32[]{:S(2)}) collective-permute-start(bf16[512,512]{1,0:T(8,128)(2,1)S(1)} %pad_maximum_fusion.2.refs_3_), channel_id=1, source_target_pairs={{0,3},{1,0},{2,1},{3,2},{4,7},{5,4},{6,5},{7,6},{8,11},{9,8},{10,9... | collective-permute-start | bytes 1572872 | tf_op jit(solution)/shard_map/ppermute | solution.py:32
  158.0 34.7 %collective-permute-start.7 = (bf16[512,512]{1,0:T(8,128)(2,1)S(1)}, bf16[512,512]{1,0:T(8,128)(2,1)S(1)}, u32[]{:S(2)}, u32[]{:S(2)}) collective-permute-start(bf16[512,512]{1,0:T(8,128)(2,1)S(1)} %pad_maximum_fusion.2.refs_3_), channel_id=1, source_target_pairs={{0,2},{1,3},{2,0},{3,1},{4,6},{5,7},{6,4},{7,5},{8,10},{9,11},{10,... | collective-permute-start | bytes 1572872 | tf_op jit(solution)/shard_map/ppermute | solution.py:32
  160.0 32.8 %collective-permute-start.6 = (bf16[512,512]{1,0:T(8,128)(2,1)S(1)}, bf16[512,512]{1,0:T(8,128)(2,1)S(1)}, u32[]{:S(2)}, u32[]{:S(2)}) collective-permute-start(bf16[512,512]{1,0:T(8,128)(2,1)S(1)} %pad_maximum_fusion.2.refs_3_), channel_id=1, source_target_pairs={{0,1},{1,2},{2,3},{3,0},{4,5},{5,6},{6,7},{7,4},{8,9},{9,10},{10,1... | collective-permute-start | bytes 1572872 | tf_op jit(solution)/shard_map/ppermute | solution.py:32
